TPU v7x, 128 devices: a whole 4x4x4 slice. The times are simulated.
128 devices in a mesh: queue: 32 (over y, z, core), batch: 4 (over x).
Axes of the slice: x: 4, y: 4, z: 4, core: 2. Of those that a mesh axis runs over, the one named last changes fastest.
Arguments:
- queries: bfloat16 [16384, 256], P(('queue', 'batch')), may hold values from -160 to 160
- keys: bfloat16 [16384, 256], P(('queue', 'batch')), may hold values from -0.5 to 0.5
- queue_keys: bfloat16 [131072, 256], P('queue'), may hold values from -2 to 2
- log_scale: float32 [1], replicated, may hold values from 0 to 1
- write_pointer: int32 [1], replicated, may hold values from 0 to 1023
- block_order: int32 [128], replicated, may hold values from 0 to 127, each once
- pos_index: int32 [16384], P(('queue', 'batch')), may hold values from 0 to 127
Outputs:
- loss: float32 [16384], P(('queue', 'batch'))
- temp_grad: float32 [1], replicated
- new_queue: bfloat16 [131072, 256], P('queue')
Inputs may be any that keep to these rules, and one draw needn't show every extreme that they name: `block_order`: each number of 0 to 127 appears once.
All inputs are finite; a program needn't handle non-finite values.
Results may differ from a plain program's by a relative error of at most 0.0004.
Values may be sent and summed in bfloat16 or wider, within the bound.
A program may use at most 64 MiB of HBM per device.

v0:
```python
import functools

import jax
import jax.numpy as jnp
from jax import lax
from jax.sharding import Mesh
from jax.sharding import PartitionSpec as P

BLOCK = 128
QUEUE = ("queue_0", "queue_1", "queue_2")
QUEUE_BATCH = ("queue_0", "queue_1", "queue_2", "batch")


def from_everyone(shard, axis):
    peers = lax.axis_size(axis)
    return lax.all_to_all(
        jnp.broadcast_to(shard[None], (peers, *shard.shape)), axis, 0, 0, tiled=True
    )


def laid_out(pieces, dim):
    pieces = jnp.moveaxis(pieces, 0, dim)
    shape = pieces.shape
    return pieces.reshape(*shape[:dim], shape[dim] * shape[dim + 1], *shape[dim + 2 :])


def gathered_copies(shard, axis, dim):
    pieces = from_everyone(shard, axis)
    return laid_out(pieces, dim)


def gathered_once(shard, axis):
    leaves = jax.tree.leaves(shard)
    turns = sorted(range(len(leaves)), key=lambda k: -leaves[k].size)
    width = (1, *leaves[turns[0]].shape)[-1]
    lines = [
        jnp.pad(leaves[k].reshape(-1), (0, -leaves[k].size % width)).reshape(-1, width)
        for k in turns
    ]
    both, at, found = (lax.all_gather(jnp.concatenate(lines), axis), 0, {})
    for k, line in zip(turns, lines):
        slab = both[:, at : at + len(line)].reshape(len(both), -1)
        found[k] = slab[:, : leaves[k].size].reshape(-1, *leaves[k].shape)
        at += len(line)
    numbers = iter(range(len(leaves)))
    return jax.tree.map(lambda _: found[next(numbers)], shard)


def joined_all(shard, axes, combine):
    for axis in axes:
        pieces = gathered_once(shard, axis)
        shard = jax.tree.map(lambda part: part[0], pieces)
        for k in range(1, lax.axis_size(axis)):
            shard = combine(shard, jax.tree.map(lambda part: part[k], pieces))
    return shard


def by_axis(shard, axes):
    return functools.reduce(lax.psum, axes, shard)


def combine(first, second):
    highest = jnp.maximum(first[0], second[0])
    first_factor = jnp.exp(first[0] - highest)
    second_factor = jnp.exp(second[0] - highest)
    return (
        highest,
        first[1] * first_factor + second[1] * second_factor,
        first[2] * first_factor + second[2] * second_factor,
    )


def block_stats(query_block, shard_keys, scale):
    logits = scale * lax.dot_general(
        query_block, shard_keys, (((1,), (1,)), ((), ())), preferred_element_type=jnp.float32
    )
    highest = jnp.max(logits, axis=1)
    weights = jnp.exp(logits - highest[:, None])
    return (highest, jnp.sum(weights, axis=1), jnp.sum(weights * logits, axis=1))


def per_device(queries, keys, queue_keys, log_scale, write_pointer, block_order, pos_index):
    scale = jnp.exp(log_scale[0])
    tok_rows = queries.shape[0]
    width = queries.shape[1]
    group_size = lax.axis_size(QUEUE)
    my_index = lax.axis_index(QUEUE)
    gathered_rows = tok_rows * group_size

    def absorb(piece):
        count = piece.shape[0]
        blocks = piece.reshape(count // 512, 512, width)
        stats = lax.map(lambda block_rows: block_stats(block_rows, queue_keys, scale), blocks)
        stats = tuple((item.reshape(count) for item in stats))
        return tuple((fresh for fresh in stats))

    peak, total, weighted = absorb(gathered_copies(queries, QUEUE, 0))
    merged = joined_all((peak, total, weighted), QUEUE, combine)
    peak, total, weighted = tuple(
        (lax.dynamic_slice_in_dim(item, my_index * tok_rows, tok_rows) for item in merged)
    )
    local_scores = lax.dot_general(
        queries, keys, (((1,), (1,)), ((), ())), preferred_element_type=jnp.float32
    )
    columns = lax.broadcasted_iota(jnp.int32, local_scores.shape, 1)
    pos = scale * jnp.sum(jnp.where(columns == pos_index[:, None], local_scores, 0.0), axis=1)
    highest = jnp.maximum(peak, pos)
    factor = jnp.exp(peak - highest)
    own_weight = jnp.exp(pos - highest)
    final_total = total * factor + own_weight
    final_weighted = weighted * factor + pos * own_weight
    lse = highest + jnp.log(final_total)
    loss = lse - pos
    terms = final_weighted / final_total - pos
    summed = by_axis(jnp.sum(terms), QUEUE_BATCH)
    temp_grad = (summed / (gathered_rows * lax.axis_size("batch"))).reshape(1)
    per_dev = queue_keys.shape[0] // BLOCK
    total_blocks = per_dev * group_size
    pointer = write_pointer[0]
    initial = queue_keys.reshape(per_dev, BLOCK, width)
    piece = lax.all_gather(keys, QUEUE_BATCH, axis=0, tiled=True)
    count = piece.shape[0] // BLOCK
    local = (pointer + block_order) % total_blocks - my_index * per_dev
    hits = local[:, None] == jnp.arange(per_dev, dtype=jnp.int32)[None, :]
    moved = jnp.einsum(
        "cs,crd->srd",
        hits.astype(jnp.bfloat16),
        piece.reshape(count, BLOCK, width),
        preferred_element_type=jnp.float32,
    ).astype(jnp.bfloat16)
    updated = jnp.where(jnp.any(hits, axis=0)[:, None, None], moved, initial)
    new_queue = updated.reshape(per_dev * BLOCK, width)
    return (loss, temp_grad, new_queue)


def solution(mesh):
    torus = Mesh(
        mesh.devices.reshape(4, 4, 2, mesh.shape["batch"]),
        ("queue_0", "queue_1", "queue_2", "batch"),
    )
    in_specs = (
        P(QUEUE_BATCH, None),
        P(QUEUE_BATCH, None),
        P(QUEUE, None),
        P(),
        P(),
        P(),
        P(QUEUE_BATCH),
    )
    out_specs = (P(QUEUE_BATCH), P(), P(QUEUE, None))
    return jax.shard_map(
        per_device, mesh=torus, in_specs=in_specs, out_specs=out_specs, check_vma=False
    )
```

profile of v0, /device:TPU:1, one launch (start us, length us, event | category | flops | bytes accessed | tf_op | source)
XLA Modules:
  0.0 175.5 jit_solution(2508819114071017730)
XLA Ops:
  9.6 9.6 %all-to-all-start = ((bf16[32,128,256]{2,1,0:T(8,128)(2,1)}), bf16[32,128,256]{2,1,0:T(8,128)(2,1)S(1)}, u32[]{:S(2)}, u32[]{:S(2)}) async-start(bf16[32,128,256]{2,1,0:T(8,128)(2,1)} %broadcast_in_dim.33), calls=%async_computation | async-start | bytes 4194304 | tf_op jit(solution)/shard_map/all_to_all | solution.py:16
  21.7 26.2 %all-to-all-done = bf16[32,128,256]{2,1,0:T(8,128)(2,1)S(1)} async-done(((bf16[32,128,256]{2,1,0:T(8,128)(2,1)}), bf16[32,128,256]{2,1,0:T(8,128)(2,1)S(1)}, u32[]{:S(2)}, u32[]{:S(2)}) %all-to-all-start) | async-done | bytes 2097184 | tf_op jit(solution)/shard_map/all_to_all | solution.py:16
  47.8 45.1 %while.14 = (s32[]{:T(128)}, f32[8,512]{1,0:T(8,128)S(1)}, f32[8,512]{1,0:T(8,128)S(1)}, f32[8,512]{1,0:T(8,128)S(1)}, f32[]{:T(128)}, /*index=5*/bf16[8,512,256...) while((s32[]{:T(128)}, f32[8,512]{1,0:T(8,128)S(1)}, f32[8,512]{1,0:T(8,128)S(1)}, ...), condition=%wide.region_4.5_spmd, body=%wide.region_0.4_spmd.sunk | while | flops 1088420352 | bytes 19157108 | solution.py:93
  47.8 3.0 %multiply_reduce_fusion.4 = (f32[512]{0:T(512)S(1)}, f32[512,4096]{1,0:T(8,128)S(1)}) fusion(f32[]{:T(128)} %get-tuple-element.150, bf16[4096,256]{1,0:T(8,128)(2,1)} %get-tuple-element.152, bf16[8,512,256]{2,1,0:T(8,128)(2,1)S(1)} %get-tuple-element.151, s32[]{:T(128)} %get-tuple-element.137), kind=kOutput, calls=%fused_computation.3.clone.1 | convolution fusion | flops 1077935616 | bytes 10749960 | tf_op jit(solution)/shard_map/while/body/eval_jaxpr/dot_general | solution.py:74
  53.4 3.0 %multiply_reduce_fusion.4 = (f32[512]{0:T(512)S(1)}, f32[512,4096]{1,0:T(8,128)S(1)}) fusion(f32[]{:T(128)} %get-tuple-element.150, bf16[4096,256]{1,0:T(8,128)(2,1)} %get-tuple-element.152, bf16[8,512,256]{2,1,0:T(8,128)(2,1)S(1)} %get-tuple-element.151, s32[]{:T(128)} %get-tuple-element.137), kind=kOutput, calls=%fused_computation.3.clone.1 | convolution fusion | flops 1077935616 | bytes 10749960 | tf_op jit(solution)/shard_map/while/body/eval_jaxpr/dot_general | solution.py:74
  56.4 2.4 %multiply_reduce_fusion.5 = (f32[512]{0:T(512)S(1)}, f32[512]{0:T(512)S(1)}) fusion(f32[512,4096]{1,0:T(8,128)S(1)} %get-tuple-element.125, f32[512]{0:T(512)S(1)} %get-tuple-element.124, f32[]{:T(128)} %get-tuple-element.150), kind=kLoop, calls=%fused_computation.clone.1 | loop fusion | flops 10484736 | bytes 8394756 | tf_op jit(solution)/shard_map/while/body/eval_jaxpr/reduce_sum | solution.py:79
  59.1 3.0 %multiply_reduce_fusion.4 = (f32[512]{0:T(512)S(1)}, f32[512,4096]{1,0:T(8,128)S(1)}) fusion(f32[]{:T(128)} %get-tuple-element.150, bf16[4096,256]{1,0:T(8,128)(2,1)} %get-tuple-element.152, bf16[8,512,256]{2,1,0:T(8,128)(2,1)S(1)} %get-tuple-element.151, s32[]{:T(128)} %get-tuple-element.137), kind=kOutput, calls=%fused_computation.3.clone.1 | convolution fusion | flops 1077935616 | bytes 10749960 | tf_op jit(solution)/shard_map/while/body/eval_jaxpr/dot_general | solution.py:74
  64.7 3.0 %multiply_reduce_fusion.4 = (f32[512]{0:T(512)S(1)}, f32[512,4096]{1,0:T(8,128)S(1)}) fusion(f32[]{:T(128)} %get-tuple-element.150, bf16[4096,256]{1,0:T(8,128)(2,1)} %get-tuple-element.152, bf16[8,512,256]{2,1,0:T(8,128)(2,1)S(1)} %get-tuple-element.151, s32[]{:T(128)} %get-tuple-element.137), kind=kOutput, calls=%fused_computation.3.clone.1 | convolution fusion | flops 1077935616 | bytes 10749960 | tf_op jit(solution)/shard_map/while/body/eval_jaxpr/dot_general | solution.py:74
  67.6 2.4 %multiply_reduce_fusion.5 = (f32[512]{0:T(512)S(1)}, f32[512]{0:T(512)S(1)}) fusion(f32[512,4096]{1,0:T(8,128)S(1)} %get-tuple-element.125, f32[512]{0:T(512)S(1)} %get-tuple-element.124, f32[]{:T(128)} %get-tuple-element.150), kind=kLoop, calls=%fused_computation.clone.1 | loop fusion | flops 10484736 | bytes 8394756 | tf_op jit(solution)/shard_map/while/body/eval_jaxpr/reduce_sum | solution.py:79
  70.3 3.0 %multiply_reduce_fusion.4 = (f32[512]{0:T(512)S(1)}, f32[512,4096]{1,0:T(8,128)S(1)}) fusion(f32[]{:T(128)} %get-tuple-element.150, bf16[4096,256]{1,0:T(8,128)(2,1)} %get-tuple-element.152, bf16[8,512,256]{2,1,0:T(8,128)(2,1)S(1)} %get-tuple-element.151, s32[]{:T(128)} %get-tuple-element.137), kind=kOutput, calls=%fused_computation.3.clone.1 | convolution fusion | flops 1077935616 | bytes 10749960 | tf_op jit(solution)/shard_map/while/body/eval_jaxpr/dot_general | solution.py:74
  73.2 2.4 %multiply_reduce_fusion.5 = (f32[512]{0:T(512)S(1)}, f32[512]{0:T(512)S(1)}) fusion(f32[512,4096]{1,0:T(8,128)S(1)} %get-tuple-element.125, f32[512]{0:T(512)S(1)} %get-tuple-element.124, f32[]{:T(128)} %get-tuple-element.150), kind=kLoop, calls=%fused_computation.clone.1 | loop fusion | flops 10484736 | bytes 8394756 | tf_op jit(solution)/shard_map/while/body/eval_jaxpr/reduce_sum | solution.py:79
  75.9 3.0 %multiply_reduce_fusion.4 = (f32[512]{0:T(512)S(1)}, f32[512,4096]{1,0:T(8,128)S(1)}) fusion(f32[]{:T(128)} %get-tuple-element.150, bf16[4096,256]{1,0:T(8,128)(2,1)} %get-tuple-element.152, bf16[8,512,256]{2,1,0:T(8,128)(2,1)S(1)} %get-tuple-element.151, s32[]{:T(128)} %get-tuple-element.137), kind=kOutput, calls=%fused_computation.3.clone.1 | convolution fusion | flops 1077935616 | bytes 10749960 | tf_op jit(solution)/shard_map/while/body/eval_jaxpr/dot_general | solution.py:74
  78.8 2.4 %multiply_reduce_fusion.5 = (f32[512]{0:T(512)S(1)}, f32[512]{0:T(512)S(1)}) fusion(f32[512,4096]{1,0:T(8,128)S(1)} %get-tuple-element.125, f32[512]{0:T(512)S(1)} %get-tuple-element.124, f32[]{:T(128)} %get-tuple-element.150), kind=kLoop, calls=%fused_computation.clone.1 | loop fusion | flops 10484736 | bytes 8394756 | tf_op jit(solution)/shard_map/while/body/eval_jaxpr/reduce_sum | solution.py:79
  81.5 3.0 %multiply_reduce_fusion.4 = (f32[512]{0:T(512)S(1)}, f32[512,4096]{1,0:T(8,128)S(1)}) fusion(f32[]{:T(128)} %get-tuple-element.150, bf16[4096,256]{1,0:T(8,128)(2,1)} %get-tuple-element.152, bf16[8,512,256]{2,1,0:T(8,128)(2,1)S(1)} %get-tuple-element.151, s32[]{:T(128)} %get-tuple-element.137), kind=kOutput, calls=%fused_computation.3.clone.1 | convolution fusion | flops 1077935616 | bytes 10749960 | tf_op jit(solution)/shard_map/while/body/eval_jaxpr/dot_general | solution.py:74
  87.1 3.2 %multiply_reduce_fusion.4 = (f32[512]{0:T(512)S(1)}, f32[512,4096]{1,0:T(8,128)S(1)}) fusion(f32[]{:T(128)} %get-tuple-element.150, bf16[4096,256]{1,0:T(8,128)(2,1)} %get-tuple-element.152, bf16[8,512,256]{2,1,0:T(8,128)(2,1)S(1)} %get-tuple-element.151, s32[]{:T(128)} %get-tuple-element.137), kind=kOutput, calls=%fused_computation.3.clone.1 | convolution fusion | flops 1077935616 | bytes 10749960 | tf_op jit(solution)/shard_map/while/body/eval_jaxpr/dot_general | solution.py:74
  93.1 9.4 %all-gather.3 = f32[4,3,4096]{2,1,0:T(4,128)S(1)} all-gather(f32[1,3,4096]{2,1,0:T(4,128)S(1)} %maximum_bitcast_fusion), channel_id=2, replica_groups=mesh['queue_0'=4,'queue_1'=4,'queue_2'=2,'batch'=4] {'queue_0'}, dimensions={0}, use_global_device_ids=true | all-gather | bytes 245760 | tf_op jit(solution)/shard_map/all_gather | solution.py:40
  102.8 9.4 %all-gather.4 = f32[4,3,4096]{2,1,0:T(4,128)S(1)} all-gather(f32[1,3,4096]{2,1,0:T(4,128)S(1)} %maximum_bitcast_fusion.1), channel_id=3, replica_groups=mesh['queue_0'=4,'queue_1'=4,'queue_2'=2,'batch'=4] {'queue_1'}, dimensions={0}, use_global_device_ids=true | all-gather | bytes 245760 | tf_op jit(solution)/shard_map/all_gather | solution.py:40
  112.6 8.0 %all-gather.5 = f32[2,3,4096]{2,1,0:T(4,128)S(1)} all-gather(f32[1,3,4096]{2,1,0:T(4,128)S(1)} %maximum_bitcast_fusion.2), channel_id=4, replica_groups=mesh['queue_0'=4,'queue_1'=4,'queue_2'=2,'batch'=4] {'queue_2'}, dimensions={0}, use_global_device_ids=true | all-gather | bytes 147456 | tf_op jit(solution)/shard_map/all_gather | solution.py:40
  121.4 6.7 %psum.28 = f32[]{:T(128)} all-reduce(f32[]{:T(128)} %get-tuple-element.61), channel_id=1, replica_groups=mesh['queue_0'=4,'queue_1'=4,'queue_2'=2,'batch'=4] {'queue_0'}, use_global_device_ids=true, to_apply=%region_7.8 | all-reduce | flops 1 | bytes 8 | tf_op jit(solution)/shard_map/psum | solution.py:59
  128.8 8.4 %psum.29 = f32[]{:T(128)} all-reduce(f32[]{:T(128)} %psum.28), channel_id=1, replica_groups=mesh['queue_0'=4,'queue_1'=4,'queue_2'=2,'batch'=4] {'queue_1'}, use_global_device_ids=true, to_apply=%region_8.9 | all-reduce | flops 1 | bytes 8 | tf_op jit(solution)/shard_map/psum | solution.py:59
  137.2 7.2 %psum.30 = f32[]{:T(128)} all-reduce(f32[]{:T(128)} %psum.29), channel_id=1, replica_groups=mesh['queue_0'=4,'queue_1'=4,'queue_2'=2,'batch'=4] {'queue_2'}, use_global_device_ids=true, to_apply=%region_9.10 | all-reduce | flops 1 | bytes 8 | tf_op jit(solution)/shard_map/psum | solution.py:59
  144.5 9.2 %psum.31 = f32[]{:T(128)} all-reduce(f32[]{:T(128)} %psum.30), channel_id=1, replica_groups=mesh['queue_0'=4,'queue_1'=4,'queue_2'=2,'batch'=4] {'batch'}, use_global_device_ids=true, to_apply=%region_10.11 | all-reduce | flops 1 | bytes 8 | tf_op jit(solution)/shard_map/psum | solution.py:59
  154.9 10.1 %copy_select_fusion = bf16[32,128,256]{2,0,1:T(8,128)(2,1)S(1)} fusion(bf16[32,128,256]{2,1,0:T(8,128)(2,1)} %bitcast.305, pred[32]{0:T(512)(128)(4,1)S(1)} %fusion.47, bf16[128,128,256]{2,1,0:T(8,128)(2,1)} %bitcast.306, s32[128]{0:T(128)S(1)} %fusion.56), kind=kOutput, calls=%fused_computation.10 | convolution fusion | flops 270536704 | bytes 12583456 | tf_op jit(solution)/shard_map/cs,crd->srd/dot_general | solution.py:125
  165.1 2.5 %copy.15 = bf16[32,128,256]{2,1,0:T(8,128)(2,1)} copy(bf16[32,128,256]{2,0,1:T(8,128)(2,1)S(1)} %copy_select_fusion) | data formatting | bytes 4194304 | tf_op jit(solution)/shard_map/jit(_where)/select_n | solution.py:131
  (55 shorter events, 17.7 us)
Async XLA Ops:
  9.6 38.3 %all-to-all-start = ((bf16[32,128,256]{2,1,0:T(8,128)(2,1)}), bf16[32,128,256]{2,1,0:T(8,128)(2,1)S(1)}, u32[]{:S(2)}, u32[]{:S(2)}) async-start(bf16[32,128,256]{2,1,0:T(8,128)(2,1)} %broadcast_in_dim.33), calls=%async_computation | async-start | bytes 4194304 | tf_op jit(solution)/shard_map/all_to_all | solution.py:16
  19.2 135.8 %all-gather.8.cloned.1.call-start = ((), (), s32[]{:S(2)}) async-start(), calls=%async_computation.1 | async-start | bytes 8454144 | tf_op jit(solution)/shard_map/all_gather | solution.py:121
  47.8 89.4 %copy-start = (s32[128]{0:T(128)S(1)}, s32[128]{0:T(128)}, u32[]{:S(2)}) copy-start(s32[128]{0:T(128)} %param.14) | copy-start | bytes 1540
Sparse Core Ops, SparseCore 0:
  23.1 75.0 all-gather.7
where the time goes:
time: 177 us; the launch traced here: 176 us
  blocking collectives  58.2 us (33%)
  matrix products  35.1 us (20%)
  waiting for transfers between devices  26.8 us (15%)
  other arithmetic  21.6 us (12%)
  between operations  17.3 us (10%)
  starting transfers between devices  9.63 us (5%)
  local copies, waits for them, and re-layouts  6.49 us (4%)
    psum x4, blocking collectives, by_axis(): return functools.reduce(lax.psum, axes, shard)  31.5 us
    all_gather x3, blocking collectives, gathered_once(): both, at, found = (lax.all_gather(jnp.concatenate(lines), axis), 0, {})  26.8 us
    all_to_all x1, waiting for transfers between devices, from_everyone(): lax.all_to_all(jnp.broadcast_to(shard[None], (peers, *shard.shape)), axis...  26.2 us
    dot_general x8, matrix products, block_stats(): lax.dot_general(query_block, shard_keys, (((1,), (1,)), ((), ())), prefer...  24 us
    reduce_sum x8, other arithmetic, block_stats(): jnp.sum(weights * logits, axis=1)  19.4 us
    dot_general x1, matrix products, per_device(): jnp.einsum('cs,crd->srd', hits.astype(jnp.bfloat16), piece.reshape(count,...  10.1 us
    all_to_all x1, starting transfers between devices, from_everyone(): lax.all_to_all(jnp.broadcast_to(shard[None], (peers, *shard.shape)), axis...  9.59 us
  transfers between devices with their start and end apart: 2, of which 1 were waited for; matrix products, arithmetic and copies ran while one was open for 27% of the time, Pallas kernels for 0%

commit v1 on v0

v1 whole, which is shorter than its diff:
```python
import functools

import jax
import jax.numpy as jnp
from jax import lax
from jax.experimental import pallas as pl
from jax.experimental.pallas import tpu as pltpu
from jax.sharding import Mesh
from jax.sharding import PartitionSpec as P

MESH = pl.DeviceIdType.MESH
ALL = ("y", "z", "c", "x")
QUEUE = ("y", "z", "c")
TOK = 128
WIDTH = 256
SLOTS = 4096
TOTAL = 16384
CHUNK = 1024
STEPS = 2 * SLOTS // CHUNK
LOG2E = 1.4426950408889634
COLORS = ((("x", "z", "y"), 0, 32), (("x", "y", "z"), 32, 32), (("z", "y", "x"), 64, 64))


def mod(value, n):
    return lax.rem(value, n)


def merge(peaks, totals, weights, c):
    peak = jnp.max(peaks, axis=0, keepdims=True)
    down = peaks - peak
    factor = jnp.exp2(down * c)
    total = jnp.sum(totals * factor, axis=0, keepdims=True)
    weight = jnp.sum((weights + down * totals) * factor, axis=0, keepdims=True)
    return peak, total, weight


def kernel(
    q_in, k_in, queue_in, log_scale, pointer, order, pos_index,
    loss_ref, grad_ref, new_ref,
    keys, qs, pool, logits, peaks, stats_out, stats_in, sums_a, sums_b, picked,
    load_sem, pair_send, pair_recv, q1_send, q1_recv, q2_send, q2_recv,
    key_send, key_recv, fwd_send, fwd_recv, st_send, st_recv, a_send, a_recv, b_send, b_recv,
):
    at = {name: lax.axis_index(name) for name in ALL}
    y, z, core, x = at["y"], at["z"], at["c"], at["x"]
    odd = mod(y + z, 2)

    def peer(**moves):
        return {name: mod(at[name] + move, 2 if name == "c" else 4) for name, move in moves.items()}

    def remote(src, dst, send, recv, device):
        return pltpu.make_async_remote_copy(
            src_ref=src, dst_ref=dst, send_sem=send, recv_sem=recv, device_id=device, device_id_type=MESH
        )

    own_q = qs.at[odd, y * (1 - odd) + z * odd, lax.div(z * (1 - odd) + y * odd, 2)]
    own_k = pool.at[y, z, core, x]
    loads = [
        pltpu.make_async_copy(q_in, own_q, load_sem.at[0]),
        pltpu.make_async_copy(k_in, own_k, load_sem.at[1]),
        pltpu.make_async_copy(queue_in, keys.at[pl.ds(0, SLOTS)], load_sem.at[2]),
    ]
    for copy in loads:
        copy.start()

    barrier = pltpu.get_barrier_semaphore()
    near = [peer(**{name: move}) for name in "xyz" for move in (1, 2, 3)] + [peer(c=1)]
    for device in near:
        pl.semaphore_signal(barrier, inc=1, device_id=device, device_id_type=MESH)
    pl.semaphore_wait(barrier, len(near))

    q1 = []
    for k in (1, 3, 2):
        q1.append(
            remote(q_in, own_q, q1_send.at[k], q1_recv.at[k], peer(y=k * odd, z=k * (1 - odd)))
        )
        q1[-1].start()
    pair = []
    for part in range(4):
        rows = pl.ds(part * 1024, 1024)
        pair.append(
            remote(
                queue_in.at[rows], keys.at[pl.ds(SLOTS + part * 1024, 1024)],
                pair_send.at[part], pair_recv.at[part], peer(c=1),
            )
        )
        pair[-1].start()

    def piece(color, free, **index):
        rings, row, count = COLORS[color]
        spot = []
        for name in "yzcx":
            if name in free:
                spot.append(slice(None))
            else:
                spot.append(index.get(name, at[name]))
        return pool.at[(*spot, pl.ds(index.get("row", row), index.get("count", count)))]

    sent = list(q1) + list(pair)

    def key_stage(color, stage):
        rings, row, count = COLORS[color]
        ring, free = rings[stage], rings[:stage]
        moves = (1, 3, 2) if stage < 2 else (1, 3)
        return [
            remote(
                k_in.at[pl.ds(row, count)] if stage == 0 else piece(color, free),
                piece(color, free),
                key_send.at[color, stage, k], key_recv.at[color, stage, k], peer(**{ring: k}),
            )
            for k in moves
        ]

    def key_last(color):
        rings, row, count = COLORS[color]
        ring, free = rings[2], rings[:2]
        half = count // 2
        copies = []
        for k, first in ((1, row), (3, row + half)):
            part = piece(color, free, **{ring: mod(at[ring] + 4 - k, 4), "row": first, "count": half})
            copies.append(
                remote(part, part, key_send.at[color, 3, k], key_recv.at[color, 3, k], peer(**{ring: k}))
            )
        return copies

    def arrivals(color, stage):
        rings, row, count = COLORS[color]
        if stage == 3:
            ring, free = rings[2], rings[:2]
            half = count // 2
            out = []
            for k, first in ((1, row), (3, row + half)):
                part = piece(color, free, **{ring: mod(at[ring] + 2, 4), "row": first, "count": half})
                out.append(remote(part, part, key_send.at[color, 3, k], key_recv.at[color, 3, k], peer(c=1)))
            return out
        ring, free = rings[stage], rings[:stage]
        moves = (1, 3, 2) if stage < 2 else (1, 3)
        out = []
        for k in moves:
            part = piece(color, free, **{ring: mod(at[ring] + 4 - k, 4)})
            out.append(remote(part, part, key_send.at[color, stage, k], key_recv.at[color, stage, k], peer(c=1)))
        return out

    def forward(color, group):
        rings, row, count = COLORS[color]
        ring, free = rings[2], rings[:2]
        move = (0, 3, 1, 2)[group]
        part = piece(color, free, **{ring: mod(at[ring] + move, 4)})
        return remote(part, part, fwd_send.at[color, group], fwd_recv.at[color, group], peer(c=1))

    def forwarded(color, group):
        rings, row, count = COLORS[color]
        ring, free = rings[2], rings[:2]
        move = (0, 3, 1, 2)[group]
        part = piece(color, free, **{ring: mod(at[ring] + move, 4), "c": 1 - core})
        return remote(part, part, fwd_send.at[color, group], fwd_recv.at[color, group], peer(c=1))

    for color in range(3):
        for copy in key_stage(color, 0):
            copy.start()
    sent += [copy for color in range(3) for copy in key_stage(color, 0)]

    scale = jnp.exp(jnp.full((1, TOK), log_scale[0], jnp.float32))
    c = scale * LOG2E
    c4 = jnp.concatenate([c] * 4, axis=1)

    lanes = lax.broadcasted_iota(jnp.int32, (1, TOK), 1)
    first_slot = ((y * 4 + z) * 2 + core) * 32
    for j in range(32):
        offset = lax.rem(first_slot + j + 1024 - pointer[0], 1024)
        picked[j] = jnp.max(jnp.where(order[...] == offset, lanes, 0))

    for copy in loads[:2]:
        copy.wait()
    scores = lax.dot_general(
        own_k[...], own_q[...], (((1,), (1,)), ((), ())), preferred_element_type=jnp.float32
    )
    rows = lax.broadcasted_iota(jnp.int32, (TOK, TOK), 0)
    positive = jnp.sum(jnp.where(rows == pos_index[...], scores, 0.0), axis=0, keepdims=True)

    def q1_spot(parity, k):
        from_y = mod(y + (4 - k) * parity, 4)
        from_z = mod(z + (4 - k) * (1 - parity), 4)
        line = from_y * (1 - parity) + from_z * parity
        return qs.at[parity, line, lax.div(from_z * (1 - parity) + from_y * parity, 2)]

    for k in (1, 2, 3):
        parity = mod(odd + k, 2)
        spot = q1_spot(parity, k)
        remote(spot, spot, q1_send.at[k], q1_recv.at[k], peer(c=1)).wait_recv()

    def q2(along, k):
        line = qs.at[0, y] if along == "y" else qs.at[1, z]
        which = 0 if along == "y" else 1
        return remote(line, line, q2_send.at[which, k], q2_recv.at[which, k], peer(**{along: k}))

    def q2_wait(k):
        for which, along in ((0, "y"), (1, "z")):
            line = qs.at[which, mod(at[along] + k, 4)]
            remote(line, line, q2_send.at[which, mod(4 - k, 4)], q2_recv.at[which, mod(4 - k, 4)], peer(c=1)).wait_recv()

    for k in (3, 1, 2):
        for along in ("y", "z"):
            q2(along, k).start()
            sent.append(q2(along, k))

    loads[2].wait()

    def tile_of(t):
        return t ^ lax.shift_right_logical(t, 1)

    def matmul(i, slot):
        t, j = lax.div(i, STEPS), lax.rem(i, STEPS)
        k = tile_of(t)
        block = keys[pl.ds(pl.multiple_of(j * CHUNK, CHUNK), CHUNK), :]
        for which, line in ((0, mod(y + k, 4)), (1, mod(z + k, 4))):
            got = lax.dot_general(
                block, qs[which, line].reshape(2 * TOK, WIDTH),
                (((1,), (1,)), ((), ())), preferred_element_type=jnp.float32,
            )
            logits[slot, :, which * 256 : which * 256 + 256] = got
            peaks[slot, :, which * 256 : which * 256 + 256] = got.reshape(CHUNK // 8, 8, 256).max(0)

    def owner(k, b):
        line_y, line_z = mod(y + k, 4), mod(z + k, 4)
        if b < 2:
            return line_y, 2 * b + mod(line_y, 2)
        return 2 * (b - 2) + mod(line_z + 1, 2), line_z

    def send_stats(t, b):
        k = tile_of(t)
        own_y, own_z = owner(k, b)
        return own_y, own_z, remote(
            stats_out.at[t, b], stats_in.at[y, z], st_send.at[t, b], st_recv.at[y, z], {"y": own_y, "z": own_z}
        )

    def events(i):
        def when(step, fn):
            pl.when(i == step)(fn)

        def pair_ready():
            for copy in pair:
                copy.wait_recv()

        def keys_two():
            for color in range(3):
                for copy in arrivals(color, 0):
                    copy.wait_recv()
                for copy in key_stage(color, 1):
                    copy.start()

        def keys_three():
            for color in range(3):
                for copy in arrivals(color, 1):
                    copy.wait_recv()
                for copy in key_stage(color, 2):
                    copy.start()
                forward(color, 0).start()

        def keys_four():
            for color in range(3):
                for copy in arrivals(color, 2):
                    copy.wait_recv()
                for copy in key_last(color):
                    copy.start()
                forward(color, 1).start()
                forward(color, 2).start()

        when(0, keys_two)
        when(2, pair_ready)
        when(STEPS - 1, lambda: q2_wait(1))
        when(9, keys_three)
        when(2 * STEPS - 1, lambda: q2_wait(3))
        when(3 * STEPS - 1, lambda: q2_wait(2))
        when(24, keys_four)

    matmul(jnp.int32(0), 0)
    steps = 4 * STEPS

    def body(i2, carry):
        for parity in range(2):
            i = i2 * 2 + parity
            t, j = lax.div(i, STEPS), lax.rem(i, STEPS)
            events(i)
            m0, l0, w0 = carry
            fresh_tile = j == 0
            m0 = jnp.where(fresh_tile, -1e30, m0)
            l0 = jnp.where(fresh_tile, 0.0, l0)
            w0 = jnp.where(fresh_tile, 0.0, w0)
            matmul(jnp.minimum(i + 1, steps - 1), 1 - parity)
            m = jnp.maximum(m0, peaks[parity])
            down = logits[parity].reshape(CHUNK // 8, 8, 512) - m[None]
            p = jnp.exp2(down * c4)
            e0 = m0 - m
            a = jnp.exp2(e0 * c4)
            l1 = l0 * a + p.sum(0)
            w1 = (w0 + e0 * l0) * a + (p * down).sum(0)
            carry = (m, l1, w1)

        @pl.when(j == STEPS - 1)
        def _():
            peak, total, weight = merge(m, l1, w1, c4)
            for b in range(4):
                cut = slice(b * TOK, (b + 1) * TOK)
                stats_out[t, b, 0:1] = peak[:, cut]
                stats_out[t, b, 1:2] = total[:, cut]
                stats_out[t, b, 2:3] = weight[:, cut]
            for b in range(4):
                own_y, own_z, copy = send_stats(t, b)
                mine = jnp.logical_and(own_y == y, own_z == z)

                @pl.when(jnp.logical_not(mine))
                def _():
                    copy.start()

                @pl.when(mine)
                def _():
                    stats_in[y, z] = stats_out[t, b]

        return carry

    zero = jnp.zeros((8, 512), jnp.float32)
    lax.fori_loop(0, steps // 2, body, (zero, zero, zero))

    for dy in range(4):
        for dz in range(4):
            if dy or dz:
                sy, sz = mod(y + dy, 4), mod(z + dz, 4)
                spot = stats_in.at[sy, sz]
                remote(spot, spot, st_send.at[0, 0], st_recv.at[sy, sz], peer(c=1)).wait_recv()
    got = stats_in[...].reshape(16, 8, TOK)
    peak = jnp.maximum(jnp.max(got[:, 0], axis=0, keepdims=True), positive)
    down = got[:, 0] - peak
    factor = jnp.exp2(down * c)
    own = positive - peak
    own_weight = jnp.exp2(own * c)
    total = jnp.sum(got[:, 1] * factor, axis=0, keepdims=True) + own_weight
    weight = (
        jnp.sum((got[:, 2] + down * got[:, 1]) * factor, axis=0, keepdims=True) + own * own_weight
    )
    loss_ref[...] = jnp.log(total) - scale * own
    terms = scale * (weight / total - own)
    mine = jnp.broadcast_to(jnp.sum(terms, axis=1, keepdims=True), (8, TOK))
    sums_a[y, z] = mine
    a_copies = []
    for dy in range(4):
        for dz in range(4):
            if dy or dz:
                copy = remote(
                    sums_a.at[y, z], sums_a.at[y, z], a_send.at[dy, dz], a_recv.at[y, z], peer(y=dy, z=dz)
                )
                copy.start()
                a_copies.append(copy)

    for color in range(3):
        for copy in arrivals(color, 3):
            copy.wait_recv()
        forward(color, 3).start()

    for dy in range(4):
        for dz in range(4):
            if dy or dz:
                sy, sz = mod(y + dy, 4), mod(z + dz, 4)
                spot = sums_a.at[sy, sz]
                remote(spot, spot, a_send.at[dy, dz], a_recv.at[sy, sz], peer(c=1)).wait_recv()
    sums_b[core, x] = jnp.sum(sums_a[...].reshape(16, 8, TOK), axis=0)
    b_copies = []
    for dc in range(2):
        for dx in range(4):
            if dc or dx:
                copy = remote(
                    sums_b.at[core, x], sums_b.at[core, x], b_send.at[dc, dx], b_recv.at[core, x], peer(c=dc, x=dx)
                )
                copy.start()
                b_copies.append(copy)

    for color in range(3):
        for group in range(4):
            forwarded(color, group).wait_recv()
    for j in range(32):
        offset = lax.rem(first_slot + j + 1024 - pointer[0], 1024)
        block = picked[j]
        hit = offset < TOK
        cut = pl.ds(j * TOK, TOK)
        new = pool[block // 32, lax.rem(block // 8, 4), lax.rem(block // 4, 2), lax.rem(block, 4)]
        new_ref[cut, :] = jnp.where(hit, new, keys[cut, :])

    for dc in range(2):
        for dx in range(4):
            if dc or dx:
                sc, sx = mod(core + dc, 2), mod(x + dx, 4)
                spot = sums_b.at[sc, sx]
                remote(spot, spot, b_send.at[dc, dx], b_recv.at[sc, sx], peer(c=1)).wait_recv()
    grand = jnp.sum(sums_b[...].reshape(8, 8, TOK), axis=0)
    grad_ref[0] = grand[0, 0] * (1.0 / TOTAL)

    for copy in sent:
        copy.wait_send()
    for color in range(3):
        for stage in (1, 2):
            for copy in key_stage(color, stage):
                copy.wait_send()
        for copy in key_last(color):
            copy.wait_send()
        for group in range(4):
            forward(color, group).wait_send()
    for t in range(4):
        for b in range(4):
            own_y, own_z, copy = send_stats(jnp.int32(t), b)

            @pl.when(jnp.logical_not(jnp.logical_and(own_y == y, own_z == z)))
            def _():
                copy.wait_send()
    for copy in a_copies + b_copies:
        copy.wait_send()


def per_device(queries, keys, queue_keys, log_scale, write_pointer, block_order, pos_index):
    vmem = pl.BlockSpec(memory_space=pltpu.VMEM)
    smem = pl.BlockSpec(memory_space=pltpu.SMEM)
    anyspace = pl.BlockSpec(memory_space=pl.ANY)
    dma = pltpu.SemaphoreType.DMA
    f32, bf16 = jnp.float32, jnp.bfloat16
    loss, grad, new = pl.pallas_call(
        kernel,
        out_shape=[
            jax.ShapeDtypeStruct((1, TOK), f32),
            jax.ShapeDtypeStruct((1,), f32),
            jax.ShapeDtypeStruct((SLOTS, WIDTH), bf16),
        ],
        in_specs=[anyspace, anyspace, anyspace, smem, smem, vmem, vmem],
        out_specs=[vmem, smem, vmem],
        scratch_shapes=[
            pltpu.VMEM((2 * SLOTS, WIDTH), bf16),
            pltpu.VMEM((2, 4, 2, TOK, WIDTH), bf16),
            pltpu.VMEM((4, 4, 2, 4, TOK, WIDTH), bf16),
            pltpu.VMEM((2, CHUNK, 512), f32),
            pltpu.VMEM((2, 8, 512), f32),
            pltpu.VMEM((4, 4, 8, TOK), f32),
            pltpu.VMEM((4, 4, 8, TOK), f32),
            pltpu.VMEM((4, 4, 8, TOK), f32),
            pltpu.VMEM((2, 4, 8, TOK), f32),
            pltpu.SMEM((32,), jnp.int32),
            dma((3,)), dma((4,)), dma((4,)), dma((4,)), dma((4,)), dma((2, 4)), dma((2, 4)),
            dma((3, 4, 4)), dma((3, 4, 4)), dma((3, 4)), dma((3, 4)), dma((4, 4)), dma((4, 4)),
            dma((4, 4)), dma((4, 4)), dma((2, 4)), dma((2, 4)),
        ],
        compiler_params=pltpu.CompilerParams(
            collective_id=0, has_side_effects=True, vmem_limit_bytes=50 << 20
        ),
    )(
        queries, keys, queue_keys, log_scale, write_pointer,
        block_order.reshape(1, TOK), pos_index.reshape(1, TOK),
    )
    return loss.reshape(TOK), grad, new


def solution(mesh):
    torus = Mesh(mesh.devices.reshape(4, 4, 2, 4), ALL)
    return jax.shard_map(
        per_device,
        mesh=torus,
        in_specs=(P(ALL, None), P(ALL, None), P(QUEUE, None), P(), P(), P(), P(ALL)),
        out_specs=(P(ALL), P(), P(QUEUE, None)),
        check_vma=False,
    )
```

time: 177 us -> 79.2 us (0.45)
  Pallas kernels: 0 us -> 70.5 us
  blocking collectives: 58.2 us -> 0 us
  matrix products: 35.1 us -> 0 us
  waiting for transfers between devices: 26.8 us -> 0 us
  other arithmetic: 21.6 us -> 0 us
  between operations: 17.3 us -> 3.69 us
  starting transfers between devices: 9.63 us -> 0 us
    pallas_call x0 -> x1, Pallas kernels: none -> 70.5 us  [per_device(): pl.pallas_call(kernel, out_shape=[jax.ShapeDtypeStruct((1, TOK), f32), ja...]
    dot_general x10 -> x0, matrix products: 35.1 us -> none  [the longest x8 24 us: block_stats(): lax.dot_general(query_block, shard_keys, (((1,), (1,)), ((), ())), prefer...]
    psum x4 -> x0, blocking collectives: 31.5 us -> none  [by_axis(): return functools.reduce(lax.psum, axes, shard)]
    all_gather x3 -> x0, blocking collectives: 26.8 us -> none  [gathered_once(): both, at, found = (lax.all_gather(jnp.concatenate(lines), axis), 0, {})]
    all_to_all x1 -> x0, waiting for transfers between devices: 26.2 us -> none  [from_everyone(): lax.all_to_all(jnp.broadcast_to(shard[None], (peers, *shard.shape)), axis...]
    reduce_sum x9 -> x0, other arithmetic: 20.1 us -> none  [the longest x8 19.4 us: block_stats(): jnp.sum(weights * logits, axis=1)]
    all_to_all x1 -> x0, starting transfers between devices: 9.59 us -> none  [from_everyone(): lax.all_to_all(jnp.broadcast_to(shard[None], (peers, *shard.shape)), axis...]
    unnamed x5 -> x10, local copies, waits for them, and re-layouts: 0.06 us -> 4.82 us
  transfers between devices with their start and end apart: 2 -> 0, of which waited for: 1 -> 0; matrix products, arithmetic and copies ran while one was open for 27% -> 0% of each run, Pallas kernels for 0% -> 0%
where the time goes in v1:
time: 79.2 us; the launch traced here: 79 us
  Pallas kernels  70.5 us (89%)
  local copies, waits for them, and re-layouts  4.82 us (6%)
  between operations  3.69 us (5%)
    pallas_call x1, Pallas kernels, per_device(): pl.pallas_call(kernel, out_shape=[jax.ShapeDtypeStruct((1, TOK), f32), ja...  70.5 us
    unnamed x10, local copies, waits for them, and re-layouts  4.82 us

profile of v1, /device:TPU:1, one launch (start us, length us, event | category | flops | bytes accessed | tf_op | source)
XLA Modules:
  0.0 79.0 jit_solution(1080530066109349293)
XLA Ops:
  1.9 0.0 copy-start
  1.9 0.8 %copy-done = bf16[128,256]{1,0:T(8,128)(2,1)S(1)} copy-done((bf16[128,256]{1,0:T(8,128)(2,1)S(1)}, bf16[128,256]{1,0:T(8,128)(2,1)}, u32[]{:S(2)}) %copy-start) | copy-done | bytes 65560
  2.8 0.0 copy-start.1
  2.8 0.8 %copy-done.1 = bf16[128,256]{1,0:T(8,128)(2,1)S(1)} copy-done((bf16[128,256]{1,0:T(8,128)(2,1)S(1)}, bf16[128,256]{1,0:T(8,128)(2,1)}, u32[]{:S(2)}) %copy-start.1) | copy-done | bytes 65560
  3.6 0.0 copy-start.2
  3.6 0.7 copy-done.2
  4.3 0.0 copy-start.3
  4.3 0.7 copy-done.3
  4.9 70.5 %shard_map.94 = (f32[1,128]{1,0:T(1,128)S(1)}, f32[1]{0:T(128)}, bf16[4096,256]{1,0:T(8,128)(2,1)S(1)}) custom-call(bf16[128,256]{1,0:T(8,128)(2,1)S(1)} %copy-done, bf16[128,256]{1,0:T(8,128)(2,1)S(1)} %copy-done.1, bf16[4096,256]{1,0:T(8,128)(2,1)} %queue_in.1, f32[1]{0:T(128)S(6)} %copy.13.log_scale, s32[1]{0:T(128)S(6)} %copy.14.pointer, ...), custom_call_target="tpu_custom_call" | custom-call | tf_op jit(solution)/shard_map/pallas_call | solution.py:424
  75.4 0.5 copy.15
  76.5 1.3 %copy.17 = bf16[4096,256]{1,0:T(8,128)(2,1)} copy(bf16[4096,256]{1,0:T(8,128)(2,1)S(1)} %get-tuple-element.14) | data formatting | bytes 4194304
Async XLA Ops:
  1.9 0.8 %copy-start = (bf16[128,256]{1,0:T(8,128)(2,1)S(1)}, bf16[128,256]{1,0:T(8,128)(2,1)}, u32[]{:S(2)}) copy-start(bf16[128,256]{1,0:T(8,128)(2,1)} %q_in.1) | copy-start | bytes 196612
  2.8 0.8 %copy-start.1 = (bf16[128,256]{1,0:T(8,128)(2,1)S(1)}, bf16[128,256]{1,0:T(8,128)(2,1)}, u32[]{:S(2)}) copy-start(bf16[128,256]{1,0:T(8,128)(2,1)} %k_in.1) | copy-start | bytes 196612
  3.6 0.7 copy-start.2
  4.3 0.7 copy-start.3
